TPU v7x, 32 devices: a whole 2x2x4 slice. The times are simulated.
32 devices in a mesh: groups: 2 (over x), ctx: 16 (over z, y, core).
Axes of the slice: x: 2, y: 2, z: 4, core: 2. Of those that a mesh axis runs over, the one named last changes fastest.
Arguments:
- query: bfloat16 [8192, 1024], P(('groups', 'ctx')), parts along dimension 0, may hold values from -130 to 130, as said below
- key: bfloat16 [8192, 1024], P(('groups', 'ctx')), parts along dimension 0, may hold values from -4.5 to 4.5
- value: bfloat16 [8192, 1024], P(('groups', 'ctx')), parts along dimension 0, may hold values from -6 to 6
- cotangent: bfloat16 [8192, 1024], P(('groups', 'ctx')), parts along dimension 0, may hold values from -6 to 6
- global_ids: int32 [4], P('groups'), parts along dimension 0, may hold values from 0 to 63
- rand_owner: int32 [128, 6], P('groups'), parts along dimension 0, may hold values from 0 to 15, all different within a row; in each aligned block of 4 rows (0 to 3, 4 to 7, ...) at most 2 rows name the same one
- rand_local: int32 [128, 6], P('groups'), parts along dimension 0, may hold values from 0 to 3
Outputs:
- attended: bfloat16 [8192, 1024], P(('groups', 'ctx')), parts along dimension 0
- grad_query: bfloat16 [8192, 1024], P(('groups', 'ctx')), parts along dimension 0
- grad_key: bfloat16 [8192, 1024], P(('groups', 'ctx')), parts along dimension 0
- grad_value: bfloat16 [8192, 1024], P(('groups', 'ctx')), parts along dimension 0
There are 2 independent parts, one for each index of `groups`. A program takes and returns all parts, laid end to end along the dimension named above; each array names one. Nothing has to cross between parts.
Inputs may be any that keep to these rules, and one draw needn't show every extreme that they name: query and key are drawn together. `rand_owner`: each row names 6 different devices. In the 4 rows of one device no device is named more than 2 times, and in some device's rows some device is named exactly 2 times.
All inputs are finite; a program needn't handle non-finite values.
Results may differ from a plain program's by a relative error of at most 0.017.
Values may be sent and summed in bfloat16 or wider, within the bound.
A program may use at most 192 MiB of HBM per device.

v0:
```python
import functools

import jax
import jax.numpy as jnp
from jax import lax
from jax.experimental import pallas as pl
from jax.experimental.pallas import tpu as pltpu
from jax.sharding import PartitionSpec as P

HEAD_DIM = 64
GROUP_HEADS = 8
BLOCK = 64
GLOBALS = 2
ROUNDS = 3
KINDS = 3 + GLOBALS + ROUNDS
PAIR = 2 * HEAD_DIM
NEG_FILL = -1e30
SCALE = HEAD_DIM ** (-0.5)
MESH = pl.DeviceIdType.MESH


def lanes_joined(left, right):
    return jnp.concatenate([left, right], axis=1)


def greet(me, count):
    barrier = pltpu.get_barrier_semaphore()
    for step in range(1, count):
        peer = lax.rem(me + step, count)
        pl.semaphore_signal(barrier, inc=1, device_id={"ctx": peer}, device_id_type=MESH)
    return barrier


def attend_kernel(
    count,
    shares,
    glob_ids,
    owner_ref,
    local_ref,
    q_hbm,
    k_hbm,
    v_hbm,
    d_hbm,
    qo_got,
    acc_ref,
    glob_ref,
    rand_ref,
    kv_pack,
    qd_pack,
    kv_all,
    qd_all,
    qo_put,
    q_ref,
    k_ref,
    v_ref,
    d_ref,
    fetch,
    kv_out,
    kv_in,
    qd_out,
    qd_in,
    qo_out,
    qo_in,
):
    me = lax.axis_index("ctx")
    heads, tokens = kv_pack.shape[:2]
    blocks = tokens // BLOCK
    own_tokens = tokens // shares
    own_blocks = own_tokens // BLOCK
    all_blocks = count * blocks
    my_share = lax.rem(me, shares)

    pulls = [
        pltpu.make_async_copy(source, target, fetch.at[index])
        for index, (source, target) in enumerate(
            ((k_hbm, k_ref), (v_hbm, v_ref), (q_hbm, q_ref), (d_hbm, d_ref))
        )
    ]
    for pull in pulls:
        pull.start()
    barrier = greet(me, count)
    my_head = me // shares
    my_group = my_head // GROUP_HEADS
    my_rows = pl.ds(pl.multiple_of(my_share * own_tokens, own_tokens), own_tokens)

    def pack(left_ref, right_ref, out_ref):
        for pair in range(heads // 2):
            cols = slice(pair * PAIR, (pair + 1) * PAIR)
            left = left_ref[:, cols]
            right = right_ref[:, cols]
            out_ref[2 * pair] = lanes_joined(left[:, :HEAD_DIM], right[:, :HEAD_DIM])
            out_ref[2 * pair + 1] = lanes_joined(left[:, HEAD_DIM:], right[:, HEAD_DIM:])

    pulls[0].wait()
    pulls[1].wait()
    pack(k_ref, v_ref, kv_pack)
    acc_ref[...] = jnp.zeros_like(acc_ref)
    glob_ref[...] = jnp.zeros_like(glob_ref)
    pl.semaphore_wait(barrier, count - 1)

    def kv_copy(dest, came):
        return pltpu.make_async_remote_copy(
            src_ref=kv_pack.at[dest // shares].reshape(blocks, BLOCK, PAIR),
            dst_ref=kv_all.at[pl.ds(came * blocks, blocks)],
            send_sem=kv_out.at[dest],
            recv_sem=kv_in.at[came],
            device_id={"ctx": dest},
            device_id_type=MESH,
        )

    def qd_copy(dest, came):
        start = pl.multiple_of(lax.rem(dest, shares) * own_tokens, own_tokens)
        return pltpu.make_async_remote_copy(
            src_ref=qd_pack.at[dest // shares, pl.ds(start, own_tokens)],
            dst_ref=qd_all.at[came],
            send_sem=qd_out.at[dest],
            recv_sem=qd_in.at[came],
            device_id={"ctx": dest},
            device_id_type=MESH,
        )

    def qo_copy(dest, came):
        return pltpu.make_async_remote_copy(
            src_ref=qo_put.at[dest],
            dst_ref=qo_got.at[came],
            send_sem=qo_out.at[dest],
            recv_sem=qo_in.at[came],
            device_id={"ctx": dest},
            device_id_type=MESH,
        )

    for step in range(1, count):
        kv_copy(lax.rem(me + count - step, count), me).start()
    for part in range(blocks):
        kv_all[me * blocks + part] = kv_pack[my_head, part * BLOCK : (part + 1) * BLOCK]
    pulls[2].wait()
    pulls[3].wait()
    pack(q_ref, d_ref, qd_pack)
    qd_all[me] = qd_pack[my_head, my_rows, :]
    for step in range(1, count):
        peer = lax.rem(me + step, count)
        kv_copy(peer, peer).wait_recv()
    for step in range(1, count):
        qd_copy(lax.rem(me + count - step, count), me).start()

    lane = lax.broadcasted_iota(jnp.int32, (BLOCK, PAIR), 1)
    low = lane < HEAD_DIM
    row_lane = lax.broadcasted_iota(jnp.int32, (1, PAIR), 1)
    contract_last = (((1,), (1,)), ((), ()))
    contract_first = (((0,), (0,)), ((), ()))

    def load(peer, part):
        block = peer * blocks + my_share * own_blocks + part
        qd = qd_all[peer, part * BLOCK : (part + 1) * BLOCK, :]
        near = [lax.rem(block + all_blocks - 1, all_blocks), lax.rem(block + 1, all_blocks), block]
        places = near + [
            glob_ids[kind] for kind in range(GLOBALS)
        ] + [
            owner_ref[my_group * ROUNDS + kind, block] * blocks
            + local_ref[my_group * ROUNDS + kind, block]
            for kind in range(ROUNDS)
        ]
        kv = jnp.concatenate([kv_all[p] for p in places], axis=0)
        zero = jnp.zeros_like(qd)
        diag = jnp.concatenate(
            [jnp.where(low, qd * jnp.bfloat16(SCALE), zero), jnp.where(low, zero, qd)], axis=0
        )
        both = lax.dot_general(diag, kv, contract_last, preferred_element_type=jnp.float32)
        return block, near, qd, kv, diag, both

    def soften(block, both):
        scores = both[:BLOCK]
        bias = jnp.where(
            row_lane < BLOCK,
            jnp.where(block == 0, NEG_FILL, 0.0),
            jnp.where(block == all_blocks - 1, NEG_FILL, 0.0),
        ).astype(jnp.float32)
        scores = lanes_joined(scores[:, :PAIR] + bias, scores[:, PAIR:])
        row_max = jnp.max(scores, axis=1, keepdims=True)
        weights = jnp.exp(scores - row_max)
        probs = weights * (1.0 / jnp.sum(weights, axis=1, keepdims=True))
        return probs, probs.astype(jnp.bfloat16)

    def finish(peer, part, qd, kv, diag, both, probs, probs_b, attended):
        slot = peer * own_blocks + part
        row_dot = jnp.sum(
            jnp.where(low, 0.0, qd.astype(jnp.float32) * attended.astype(jnp.float32)),
            axis=1,
            keepdims=True,
        )
        dscore = (probs * (both[BLOCK:] - row_dot)).astype(jnp.bfloat16)
        grad_q = jnp.dot(dscore, kv, preferred_element_type=jnp.float32) * SCALE
        qo_put[peer, part * BLOCK : (part + 1) * BLOCK, :] = jnp.where(
            low, grad_q.astype(jnp.bfloat16), attended
        )
        terms = lax.dot_general(
            jnp.concatenate([dscore, probs_b], axis=0),
            diag,
            contract_first,
            preferred_element_type=jnp.float32,
        )
        width = ROUNDS * BLOCK
        rand_ref[pl.ds(pl.multiple_of(slot * width, width), width), :] = terms[
            (3 + GLOBALS) * BLOCK :
        ].astype(jnp.bfloat16)
        return terms

    def front(peer):
        stage = [load(peer, part) for part in range(own_blocks)]
        soft = [soften(block, both) for block, _, _, _, _, both in stage]
        seen = [
            jnp.dot(probs_b, kept[3], preferred_element_type=jnp.float32).astype(jnp.bfloat16)
            for kept, (_, probs_b) in zip(stage, soft)
        ]
        return [
            (near, finish(peer, part, qd, kv, diag, both, *soft[part], seen[part]))
            for part, (block, near, qd, kv, diag, both) in enumerate(stage)
        ]

    def step_of(step, carry):
        peer = lax.rem(me + step, count)

        @pl.when(step > 0)
        def _():
            qd_copy(peer, peer).wait_recv()

        done = front(peer)
        for near, terms in done:
            for kind in range(3):
                spot = pl.ds(pl.multiple_of(near[kind] * BLOCK, BLOCK), BLOCK)
                acc_ref[spot, :] += terms[kind * BLOCK : (kind + 1) * BLOCK]
        shared = [terms[3 * BLOCK : (3 + GLOBALS) * BLOCK] for _, terms in done]
        glob_ref[...] += functools.reduce(jnp.add, shared)

        @pl.when(step > 1)
        def _():
            qo_copy(lax.rem(me + step - 1, count), me).start()

        return carry

    lax.fori_loop(0, count, step_of, 0)
    qo_copy(lax.rem(me + count - 1, count), me).start()
    qo_got[me] = qo_put[me]
    for step in range(1, count):
        peer = lax.rem(me + step, count)
        kv_copy(peer, me).wait_send()
        qd_copy(peer, me).wait_send()
        qo_copy(peer, me).wait_send()
        qo_copy(peer, peer).wait_recv()


def sum_kernel(
    count,
    shares,
    blocks,
    glob_ids,
    owner_ref,
    local_ref,
    acc_in,
    glob_ref,
    rand_ref,
    qo_ref,
    gkv_ref,
    att_ref,
    gq_ref,
    acc_ref,
):
    me = lax.axis_index("ctx")
    own_blocks = blocks // shares
    first = lax.rem(me, shares) * own_blocks
    column = me // shares // GROUP_HEADS * ROUNDS
    acc_ref[...] = acc_in[...]
    for index in range(GLOBALS):
        spot = pl.ds(pl.multiple_of(glob_ids[index] * BLOCK, BLOCK), BLOCK)
        acc_ref[spot, :] += glob_ref[index * BLOCK : (index + 1) * BLOCK, :]

    def step(peer, carry):
        for part in range(own_blocks):
            block = peer * blocks + first + part
            slot = peer * own_blocks + part
            for kind in range(ROUNDS):
                place = owner_ref[column + kind, block] * blocks + local_ref[column + kind, block]
                spot = pl.ds(pl.multiple_of(place * BLOCK, BLOCK), BLOCK)
                came = pl.ds(pl.multiple_of((slot * ROUNDS + kind) * BLOCK, BLOCK), BLOCK)
                acc_ref[spot, :] += rand_ref[came, :].astype(jnp.float32)
        return carry

    lax.fori_loop(0, count, step, 0)
    gkv_ref[...] = acc_ref[...].astype(gkv_ref.dtype)
    own_tokens = qo_ref.shape[1]
    pairs = qo_ref.shape[0] // shares // 2
    for pair in range(pairs):
        cols = slice(pair * PAIR, (pair + 1) * PAIR)
        for share in range(shares):
            rows = slice(share * own_tokens, (share + 1) * own_tokens)
            even = qo_ref[2 * pair * shares + share]
            odd = qo_ref[(2 * pair + 1) * shares + share]
            gq_ref[rows, cols] = lanes_joined(even[:, :HEAD_DIM], odd[:, :HEAD_DIM])
            att_ref[rows, cols] = lanes_joined(even[:, HEAD_DIM:], odd[:, HEAD_DIM:])


def return_kernel(count, shares, gkv_ref, gk_ref, gv_ref, got, out_sem, in_sem):
    me = lax.axis_index("ctx")
    tokens = got.shape[1]
    barrier = greet(me, count)
    pl.semaphore_wait(barrier, count - 1)

    def copy(dest, came):
        return pltpu.make_async_remote_copy(
            src_ref=gkv_ref.at[dest],
            dst_ref=got.at[came],
            send_sem=out_sem.at[dest],
            recv_sem=in_sem.at[came],
            device_id={"ctx": dest},
            device_id_type=MESH,
        )

    for step in range(1, count):
        copy(lax.rem(me + count - step, count), me).start()
    got[me] = gkv_ref[me]

    def head_of(head):
        for share in range(shares):
            source = head * shares + share

            @pl.when(source != me)
            def _():
                copy(source, source).wait_recv()

        total = got[head * shares]
        if shares > 1:
            total = total.astype(jnp.float32)
            for share in range(1, shares):
                total += got[head * shares + share].astype(jnp.float32)
            total = total.astype(jnp.bfloat16)
        return total

    for pair in range(count // shares // 2):
        cols = slice(pair * PAIR, (pair + 1) * PAIR)
        even = head_of(2 * pair)
        odd = head_of(2 * pair + 1)
        gk_ref[:, cols] = lanes_joined(even[:, :HEAD_DIM], odd[:, :HEAD_DIM])
        gv_ref[:, cols] = lanes_joined(even[:, HEAD_DIM:], odd[:, HEAD_DIM:])
    for step in range(1, count):
        copy(lax.rem(me + step, count), me).wait_send()


VMEM = pl.BlockSpec(memory_space=pltpu.VMEM)
SMEM = pl.BlockSpec(memory_space=pltpu.SMEM)


def per_device(query, key, value, cotangent, global_ids, rand_owner, rand_local):
    tokens, features = query.shape
    blocks = tokens // BLOCK
    heads = features // HEAD_DIM
    count = lax.axis_size("ctx")
    shares = count // heads
    own_blocks = blocks // shares
    own_tokens = own_blocks * BLOCK
    all_blocks = count * blocks
    slots = count * own_blocks
    shape = jax.ShapeDtypeStruct
    bf16, f32 = jnp.bfloat16, jnp.float32

    dma = pltpu.SemaphoreType.DMA((count,))
    qo, acc, glob, rand = pl.pallas_call(
        functools.partial(attend_kernel, count, shares),
        out_shape=(
            shape((count, own_tokens, PAIR), bf16),
            shape((count * tokens, PAIR), f32),
            shape((GLOBALS * BLOCK, PAIR), f32),
            shape((slots * ROUNDS * BLOCK, PAIR), bf16),
        ),
        in_specs=[SMEM] * 3 + [pl.BlockSpec(memory_space=pltpu.HBM)] * 4,
        out_specs=(VMEM,) * 4,
        scratch_shapes=[
            pltpu.VMEM((heads, tokens, PAIR), bf16),
            pltpu.VMEM((heads, tokens, PAIR), bf16),
            pltpu.VMEM((all_blocks, BLOCK, PAIR), bf16),
            pltpu.VMEM((count, own_tokens, PAIR), bf16),
            pltpu.VMEM((count, own_tokens, PAIR), bf16),
        ]
        + [pltpu.VMEM((tokens, features), bf16)] * 4
        + [pltpu.SemaphoreType.DMA((4,))]
        + [dma] * 6,
        compiler_params=pltpu.CompilerParams(
            collective_id=0, has_side_effects=True, vmem_limit_bytes=40 * 1024 * 1024
        ),
        name="attend",
    )(global_ids, rand_owner.T, rand_local.T, query, key, value, cotangent)
    flat = shape((tokens, features), bf16)
    gkv, attended, grad_query = pl.pallas_call(
        functools.partial(sum_kernel, count, shares, blocks),
        out_shape=(shape((count * tokens, PAIR), bf16), flat, flat),
        in_specs=[SMEM] * 3 + [VMEM] * 4,
        out_specs=(VMEM,) * 3,
        scratch_shapes=[pltpu.VMEM((count * tokens, PAIR), f32)],
        compiler_params=pltpu.CompilerParams(vmem_limit_bytes=32 * 1024 * 1024),
        name="total",
    )(global_ids, rand_owner.T, rand_local.T, acc, glob, rand, qo)
    grad_key, grad_value = pl.pallas_call(
        functools.partial(return_kernel, count, shares),
        out_shape=(flat, flat),
        in_specs=[VMEM],
        out_specs=(VMEM,) * 2,
        scratch_shapes=[pltpu.VMEM((count, tokens, PAIR), bf16), dma, dma],
        compiler_params=pltpu.CompilerParams(
            collective_id=1, has_side_effects=True, vmem_limit_bytes=16 * 1024 * 1024
        ),
        name="back",
    )(gkv.reshape(count, tokens, PAIR))
    return attended, grad_query, grad_key, grad_value


def solution(mesh):
    rows = P(("groups", "ctx"), None)
    return jax.shard_map(
        per_device,
        mesh=mesh,
        in_specs=(rows, rows, rows, rows, P("groups"), P("groups", None), P("groups", None)),
        out_specs=(rows,) * 4,
        check_vma=False,
    )
```

profile of v0, /device:TPU:0, one launch (start us, length us, event | category | flops | bytes accessed | tf_op | source)
XLA Modules:
  0.0 128.1 jit_solution(15194038266618007503)
XLA Ops:
  0.6 0.0 copy-start
  0.6 1.0 copy-done
  1.7 0.0 copy-start.1
  1.7 1.0 copy-done.1
  2.7 0.0 copy-start.2
  2.7 1.0 copy-done.2
  3.8 0.0 copy-start.3
  3.8 1.0 copy-done.3
  4.8 0.0 copy-start.4
  4.8 0.7 copy-done.4
  5.5 0.0 copy-start.5
  5.5 0.7 copy-done.5
  6.2 0.0 copy-start.6
  6.2 0.7 copy-done.6
  6.8 82.1 %attend.1 = (bf16[16,256,128]{2,1,0:T(8,128)(2,1)S(1)}, f32[4096,128]{1,0:T(8,128)S(1)}, f32[128,128]{1,0:T(8,128)S(1)}, bf16[12288,128]{1,0:T(8,128)(2,1)S(1)}) custom-call(s32[2]{0:T(128)S(1)} %copy-done.6, s32[6,64]{1,0:T(8,128)S(1)} %bitcast.4, s32[6,64]{1,0:T(8,128)S(1)} %bitcast.6, bf16[256,1024]{1,0:T(8,128)(2,1)S(1)} %copy-done, ...), custom_call_target="tpu_custom_call" | custom-call | tf_op jit(solution)/shard_map/attend/pallas_call | solution.py:366
  88.9 3.5 %total.1 = (bf16[4096,128]{1,0:T(8,128)(2,1)S(1)}, bf16[256,1024]{1,0:T(8,128)(2,1)}, bf16[256,1024]{1,0:T(8,128)(2,1)}) custom-call(s32[2]{0:T(128)S(1)} %copy-done.6, s32[6,64]{1,0:T(8,128)S(1)} %bitcast.5, s32[6,64]{1,0:T(8,128)S(1)} %bitcast.7, f32[4096,128]{1,0:T(8,128)S(1)} %get-tuple-element.13.acc_in, f32[128,128]{1,0:T(8,128)S(1)} %get-tuple-element.14.glob_ref, ...), custom_call_target="tpu_custom_call" | custom-call | tf_op jit(solution)/shard_map/total/pallas_call | solution.py:392
  92.4 34.1 %back.1 = (bf16[256,1024]{1,0:T(8,128)(2,1)S(1)}, bf16[256,1024]{1,0:T(8,128)(2,1)S(1)}) custom-call(bf16[16,256,128]{2,1,0:T(8,128)(2,1)S(1)} %bitcast.3), custom_call_target="tpu_custom_call" | custom-call | tf_op jit(solution)/shard_map/back/pallas_call | solution.py:401
  126.5 0.8 copy.13
  127.3 0.8 copy.14
Async XLA Ops:
  0.6 1.0 copy-start
  1.7 1.0 copy-start.1
  2.7 1.0 copy-start.2
  3.8 1.0 copy-start.3
  4.8 0.7 copy-start.4
  5.5 0.7 copy-start.5
  6.2 0.7 copy-start.6
where the time goes:
time: 128 us
  Pallas kernels  120 us (94%)
  local copies, waits for them, and re-layouts  7.77 us (6%)
    pallas_call x1, Pallas kernels, per_device(): pl.pallas_call(functools.partial(attend_kernel, count, shares), out_shape...  82.1 us
    pallas_call x1, Pallas kernels, per_device(): pl.pallas_call(functools.partial(return_kernel, count, shares), out_shape...  34.1 us
    unnamed x16, local copies, waits for them, and re-layouts  7.77 us
    pallas_call x1, Pallas kernels, per_device(): pl.pallas_call(functools.partial(sum_kernel, count, shares, blocks), out_...  3.49 us

commit v1 on v0

v1 whole, which is shorter than its diff:
```python
import functools

import jax
import jax.numpy as jnp
from jax import lax
from jax.experimental import pallas as pl
from jax.experimental.pallas import tpu as pltpu
from jax.sharding import PartitionSpec as P

HEAD_DIM = 64
GROUP_HEADS = 8
BLOCK = 64
GLOBALS = 2
ROUNDS = 3
PAIR = 2 * HEAD_DIM
NEG_FILL = -1e30
SCALE = HEAD_DIM ** (-0.5)
MESH = pl.DeviceIdType.MESH


def lanes_joined(left, right):
    return jnp.concatenate([left, right], axis=1)


def fused_kernel(
    count,
    shares,
    glob_hbm,
    owner_hbm,
    local_hbm,
    q_hbm,
    k_hbm,
    v_hbm,
    d_hbm,
    att_ref,
    gq_ref,
    gk_ref,
    gv_ref,
    kv_pack,
    qd_pack,
    kv_all,
    qd_all,
    qo_put,
    qo_got,
    gkv_put,
    gkv_got,
    acc_ref,
    chain_ref,
    glob_ref,
    q_ref,
    k_ref,
    v_ref,
    d_ref,
    owner_vec,
    local_vec,
    table_vec,
    glob_ids,
    owner_ref,
    local_ref,
    table,
    fetch,
    drain,
    kv_out,
    kv_in,
    qd_out,
    qd_in,
    qo_out,
    qo_in,
    gkv_out,
    gkv_in,
):
    me = lax.axis_index("ctx")
    heads, tokens = kv_pack.shape[:2]
    blocks = tokens // BLOCK
    own_tokens = tokens // shares
    own_blocks = own_tokens // BLOCK
    all_blocks = count * blocks
    entries = count * own_blocks * ROUNDS
    my_share = lax.rem(me, shares)
    my_head = me // shares
    my_group = my_head // GROUP_HEADS
    my_rows = pl.ds(pl.multiple_of(my_share * own_tokens, own_tokens), own_tokens)

    pulls = [
        pltpu.make_async_copy(source, target, fetch.at[index])
        for index, (source, target) in enumerate(
            (
                (k_hbm, k_ref),
                (v_hbm, v_ref),
                (q_hbm, q_ref),
                (d_hbm, d_ref),
                (owner_hbm, owner_ref),
                (local_hbm, local_ref),
                (owner_hbm, owner_vec),
                (local_hbm, local_vec),
                (glob_hbm, glob_ids),
            )
        )
    ]
    for pull in pulls:
        pull.start()
    barrier = pltpu.get_barrier_semaphore()
    for step in range(1, count):
        peer = lax.rem(me + step, count)
        pl.semaphore_signal(barrier, inc=1, device_id={"ctx": peer}, device_id_type=MESH)

    def pack(left_ref, right_ref, out_ref):
        for pair in range(heads // 2):
            cols = slice(pair * PAIR, (pair + 1) * PAIR)
            left = left_ref[:, cols]
            right = right_ref[:, cols]
            out_ref[2 * pair] = lanes_joined(left[:, :HEAD_DIM], right[:, :HEAD_DIM])
            out_ref[2 * pair + 1] = lanes_joined(left[:, HEAD_DIM:], right[:, HEAD_DIM:])

    pulls[0].wait()
    pulls[1].wait()
    pack(k_ref, v_ref, kv_pack)
    pulls[2].wait()
    pulls[3].wait()
    pack(q_ref, d_ref, qd_pack)
    pl.semaphore_wait(barrier, count - 1)

    def kv_copy(dest, came):
        return pltpu.make_async_remote_copy(
            src_ref=kv_pack.at[dest // shares].reshape(blocks, BLOCK, PAIR),
            dst_ref=kv_all.at[pl.ds(came * blocks, blocks)],
            send_sem=kv_out.at[dest],
            recv_sem=kv_in.at[came],
            device_id={"ctx": dest},
            device_id_type=MESH,
        )

    def qd_copy(dest, came):
        start = pl.multiple_of(lax.rem(dest, shares) * own_tokens, own_tokens)
        return pltpu.make_async_remote_copy(
            src_ref=qd_pack.at[dest // shares, pl.ds(start, own_tokens)],
            dst_ref=qd_all.at[came],
            send_sem=qd_out.at[dest],
            recv_sem=qd_in.at[came],
            device_id={"ctx": dest},
            device_id_type=MESH,
        )

    def row_copy(put_ref, got_ref, out_sem, in_sem):
        def copy(dest, came):
            return pltpu.make_async_remote_copy(
                src_ref=put_ref.at[dest],
                dst_ref=got_ref.at[came],
                send_sem=out_sem.at[dest],
                recv_sem=in_sem.at[came],
                device_id={"ctx": dest},
                device_id_type=MESH,
            )

        return copy

    qo_copy = row_copy(qo_put, qo_got, qo_out, qo_in)
    gkv_copy = row_copy(gkv_put, gkv_got, gkv_out, gkv_in)

    for step in range(1, count):
        kv_copy(lax.rem(me + count - step, count), me).start()
    for step in range(1, count):
        qd_copy(lax.rem(me + count - step, count), me).start()

    for part in range(blocks):
        kv_all[me * blocks + part] = kv_pack[my_head, part * BLOCK : (part + 1) * BLOCK]
    qd_all[me] = qd_pack[my_head, my_rows, :]
    acc_ref[...] = jnp.zeros_like(acc_ref)
    glob_ref[...] = jnp.zeros_like(glob_ref)
    chain_ref[entries] = jnp.zeros_like(chain_ref[entries])

    for pull in pulls[4:]:
        pull.wait()
    first_row = my_group * ROUNDS
    rows = pl.ds(first_row, ROUNDS)
    places = owner_vec[rows, :] * blocks + local_vec[rows, :]
    block_of = lax.broadcasted_iota(jnp.int32, (ROUNDS, all_blocks), 1)
    round_of = lax.broadcasted_iota(jnp.int32, (ROUNDS, all_blocks), 0)
    turn = lax.rem(lax.div(block_of, blocks) + (count - me), count)
    part_of = lax.rem(block_of, blocks) - my_share * own_blocks
    order = (turn * own_blocks + part_of) * ROUNDS + round_of
    order = jnp.where((part_of >= 0) & (part_of < own_blocks), order, -1)
    lane_block = lax.broadcasted_iota(jnp.int32, (1, all_blocks), 1)

    def link(step, carry):
        before, last = carry
        peer = lax.rem(me + step, count)
        for part in range(own_blocks):
            block = peer * blocks + my_share * own_blocks + part
            for kind in range(ROUNDS):
                entry = (step * own_blocks + part) * ROUNDS + kind
                place = (
                    owner_ref[first_row + kind, block] * blocks + local_ref[first_row + kind, block]
                )
                before = jnp.where((places == place) & (order > entry), entry, before)
                last = jnp.where(lane_block == place, entry, last)
        return before, last

    before, last = lax.fori_loop(
        0,
        count,
        link,
        (
            jnp.full((ROUNDS, all_blocks), entries, jnp.int32),
            jnp.full((1, all_blocks), entries, jnp.int32),
        ),
    )
    which = jnp.zeros((1, all_blocks), jnp.int32)
    for index in range(GLOBALS):
        which += jnp.where(lane_block == glob_ids[index], 1 << index, 0)
    table_vec[0:ROUNDS, :] = places
    table_vec[ROUNDS : 2 * ROUNDS, :] = before
    table_vec[2 * ROUNDS : 2 * ROUNDS + 1, :] = last
    table_vec[2 * ROUNDS + 1 : 2 * ROUNDS + 2, :] = which
    to_scalar = pltpu.make_async_copy(table_vec, table, fetch.at[len(pulls)])
    to_scalar.start()
    to_scalar.wait()

    for step in range(1, count):
        peer = lax.rem(me + step, count)
        kv_copy(peer, peer).wait_recv()

    lane = lax.broadcasted_iota(jnp.int32, (BLOCK, PAIR), 1)
    low = lane < HEAD_DIM
    row_lane = lax.broadcasted_iota(jnp.int32, (1, PAIR), 1)
    contract_last = (((1,), (1,)), ((), ()))
    contract_first = (((0,), (0,)), ((), ()))

    def load(peer, part):
        block = peer * blocks + my_share * own_blocks + part
        qd = qd_all[peer, part * BLOCK : (part + 1) * BLOCK, :]
        near = [lax.rem(block + all_blocks - 1, all_blocks), lax.rem(block + 1, all_blocks), block]
        spots = near + [glob_ids[kind] for kind in range(GLOBALS)]
        spots = spots + [table[kind, block] for kind in range(ROUNDS)]
        kv = jnp.concatenate([kv_all[p] for p in spots], axis=0)
        zero = jnp.zeros_like(qd)
        diag = jnp.concatenate(
            [jnp.where(low, qd * jnp.bfloat16(SCALE), zero), jnp.where(low, zero, qd)], axis=0
        )
        both = lax.dot_general(diag, kv, contract_last, preferred_element_type=jnp.float32)
        return block, near, qd, kv, diag, both

    def soften(block, both):
        scores = both[:BLOCK]
        bias = jnp.where(
            row_lane < BLOCK,
            jnp.where(block == 0, NEG_FILL, 0.0),
            jnp.where(block == all_blocks - 1, NEG_FILL, 0.0),
        ).astype(jnp.float32)
        scores = lanes_joined(scores[:, :PAIR] + bias, scores[:, PAIR:])
        row_max = jnp.max(scores, axis=1, keepdims=True)
        weights = jnp.exp(scores - row_max)
        probs = weights * (1.0 / jnp.sum(weights, axis=1, keepdims=True))
        return probs, probs.astype(jnp.bfloat16)

    def finish(peer, step, part, block, qd, kv, diag, both, probs, probs_b, attended):
        row_dot = jnp.sum(
            jnp.where(low, 0.0, qd.astype(jnp.float32) * attended.astype(jnp.float32)),
            axis=1,
            keepdims=True,
        )
        dscore = (probs * (both[BLOCK:] - row_dot)).astype(jnp.bfloat16)
        grad_q = jnp.dot(dscore, kv, preferred_element_type=jnp.float32) * SCALE
        qo_put[peer, part * BLOCK : (part + 1) * BLOCK, :] = jnp.where(
            low, grad_q.astype(jnp.bfloat16), attended
        )
        terms = lax.dot_general(
            jnp.concatenate([dscore, probs_b], axis=0),
            diag,
            contract_first,
            preferred_element_type=jnp.float32,
        )
        return terms

    def front(peer, step):
        stage = [load(peer, part) for part in range(own_blocks)]
        soft = [soften(block, both) for block, _, _, _, _, both in stage]
        seen = [
            jnp.dot(probs_b, kept[3], preferred_element_type=jnp.float32).astype(jnp.bfloat16)
            for kept, (_, probs_b) in zip(stage, soft)
        ]
        return [
            (
                block,
                near,
                finish(peer, step, part, block, qd, kv, diag, both, *soft[part], seen[part]),
            )
            for part, (block, near, qd, kv, diag, both) in enumerate(stage)
        ]

    def step_of(step, carry):
        peer = lax.rem(me + step, count)

        @pl.when(step > 0)
        def _():
            qd_copy(peer, peer).wait_recv()

        done = front(peer, step)
        for part, (block, near, terms) in enumerate(done):
            for kind in range(3):
                spot = pl.ds(pl.multiple_of(near[kind] * BLOCK, BLOCK), BLOCK)
                acc_ref[spot, :] += terms[kind * BLOCK : (kind + 1) * BLOCK]
            for kind in range(ROUNDS):
                start = (3 + GLOBALS + kind) * BLOCK
                term = terms[start : start + BLOCK].astype(jnp.bfloat16).astype(jnp.float32)
                entry = (step * own_blocks + part) * ROUNDS + kind
                chain_ref[entry] = chain_ref[table[ROUNDS + kind, block]] + term
        shared = functools.reduce(
            jnp.add, [terms[3 * BLOCK : (3 + GLOBALS) * BLOCK] for _, _, terms in done]
        )
        for index in range(GLOBALS):
            own = shared[index * BLOCK : (index + 1) * BLOCK]
            for mix in range(1, 1 << GLOBALS):
                if mix >> index & 1:
                    glob_ref[mix] += own

        @pl.when(step > 1)
        def _():
            qo_copy(lax.rem(me + step - 1, count), me).start()

        return carry

    lax.fori_loop(0, count, step_of, 0)
    qo_copy(lax.rem(me + count - 1, count), me).start()

    def total_of(step, carry):
        dest = lax.rem(me + count - step, count)
        for part in range(blocks):
            block = dest * blocks + part
            spot = pl.ds(pl.multiple_of(block * BLOCK, BLOCK), BLOCK)
            total = acc_ref[spot, :] + chain_ref[table[2 * ROUNDS, block]]
            total = total + glob_ref[table[2 * ROUNDS + 1, block]]
            gkv_put[dest, part * BLOCK : (part + 1) * BLOCK, :] = total.astype(jnp.bfloat16)

        @pl.when(step > 0)
        def _():
            gkv_copy(dest, me).start()

        return carry

    lax.fori_loop(0, count, total_of, 0)
    qo_got[me] = qo_put[me]
    gkv_got[me] = gkv_put[me]

    for step in range(1, count):
        peer = lax.rem(me + step, count)
        qo_copy(peer, peer).wait_recv()
    for pair in range(heads // 2):
        cols = slice(pair * PAIR, (pair + 1) * PAIR)
        for share in range(shares):
            part = slice(share * own_tokens, (share + 1) * own_tokens)
            even = qo_got[2 * pair * shares + share]
            odd = qo_got[(2 * pair + 1) * shares + share]
            q_ref[part, cols] = lanes_joined(even[:, :HEAD_DIM], odd[:, :HEAD_DIM])
            d_ref[part, cols] = lanes_joined(even[:, HEAD_DIM:], odd[:, HEAD_DIM:])
    pushes = [
        pltpu.make_async_copy(source, target, fetch.at[place])
        for place, (source, target) in enumerate(((q_ref, gq_ref), (d_ref, att_ref)))
    ]
    for push in pushes:
        push.start()
    for step in range(1, count):
        peer = lax.rem(me + step, count)
        kv_copy(peer, me).wait_send()
        qd_copy(peer, me).wait_send()
        qo_copy(peer, me).wait_send()

    def head_of(head):
        for share in range(shares):
            source = head * shares + share

            @pl.when(source != me)
            def _():
                gkv_copy(source, source).wait_recv()

        total = gkv_got[head * shares]
        if shares > 1:
            total = total.astype(jnp.float32)
            for share in range(1, shares):
                total += gkv_got[head * shares + share].astype(jnp.float32)
            total = total.astype(jnp.bfloat16)
        return total

    for pair in range(heads // 2):
        cols = slice(pair * PAIR, (pair + 1) * PAIR)
        even = head_of(2 * pair)
        odd = head_of(2 * pair + 1)
        k_ref[:, cols] = lanes_joined(even[:, :HEAD_DIM], odd[:, :HEAD_DIM])
        v_ref[:, cols] = lanes_joined(even[:, HEAD_DIM:], odd[:, HEAD_DIM:])
        for place, (source, target) in enumerate(((k_ref, gk_ref), (v_ref, gv_ref))):
            push = pltpu.make_async_copy(
                source.at[:, cols], target.at[:, cols], drain.at[place, pair]
            )
            push.start()
            pushes.append(push)
    for step in range(1, count):
        gkv_copy(lax.rem(me + step, count), me).wait_send()
    for push in pushes:
        push.wait()


def store_kernel(*refs):
    size = (len(refs) - 3) // 2
    hold, come, go = refs[2 * size :]
    half = hold.shape[1] // 2
    pulls, pushes = [], []
    for index in range(size):
        for part in range(2):
            rows = pl.ds(part * half, half)
            here = hold.at[index, rows]
            pulls.append(pltpu.make_async_copy(refs[index].at[rows], here, come.at[index, part]))
            pushes.append(
                pltpu.make_async_copy(here, refs[size + index].at[rows], go.at[index, part])
            )
    for pull in pulls:
        pull.start()
    for pull, push in zip(pulls, pushes):
        pull.wait()
        push.start()
    for push in pushes:
        push.wait()


HBM = pl.BlockSpec(memory_space=pltpu.HBM)


def per_device(query, key, value, cotangent, global_ids, rand_owner, rand_local):
    tokens, features = query.shape
    blocks = tokens // BLOCK
    heads = features // HEAD_DIM
    count = lax.axis_size("ctx")
    shares = count // heads
    own_blocks = blocks // shares
    own_tokens = own_blocks * BLOCK
    all_blocks = count * blocks
    entries = count * own_blocks * ROUNDS
    shape = jax.ShapeDtypeStruct
    bf16, f32, i32 = jnp.bfloat16, jnp.float32, jnp.int32

    dma = pltpu.SemaphoreType.DMA((count,))
    flat = shape((tokens, features), bf16)
    whole = pltpu.VMEM((tokens, features), bf16)
    index = (rand_owner.shape[1], all_blocks)
    results = pl.pallas_call(
        functools.partial(fused_kernel, count, shares),
        out_shape=(flat,) * 4,
        in_specs=[HBM] * 7,
        out_specs=(HBM,) * 4,
        scratch_shapes=[
            pltpu.VMEM((heads, tokens, PAIR), bf16),
            pltpu.VMEM((heads, tokens, PAIR), bf16),
            pltpu.VMEM((all_blocks, BLOCK, PAIR), bf16),
            pltpu.VMEM((count, own_tokens, PAIR), bf16),
            pltpu.VMEM((count, own_tokens, PAIR), bf16),
            pltpu.VMEM((count, own_tokens, PAIR), bf16),
            pltpu.VMEM((count, tokens, PAIR), bf16),
            pltpu.VMEM((count, tokens, PAIR), bf16),
            pltpu.VMEM((count * tokens, PAIR), f32),
            pltpu.VMEM((entries + 1, BLOCK, PAIR), f32),
            pltpu.VMEM((1 << GLOBALS, BLOCK, PAIR), f32),
            whole,
            whole,
            whole,
            whole,
            pltpu.VMEM(index, i32),
            pltpu.VMEM(index, i32),
            pltpu.VMEM((2 * ROUNDS + 2, all_blocks), i32),
            pltpu.SMEM((GLOBALS,), i32),
            pltpu.SMEM(index, i32),
            pltpu.SMEM(index, i32),
            pltpu.SMEM((2 * ROUNDS + 2, all_blocks), i32),
            pltpu.SemaphoreType.DMA((10,)),
            pltpu.SemaphoreType.DMA((2, heads // 2)),
        ]
        + [dma] * 8,
        compiler_params=pltpu.CompilerParams(
            collective_id=0, has_side_effects=True, vmem_limit_bytes=60 * 1024 * 1024
        ),
        name="attend",
    )(global_ids, rand_owner.T, rand_local.T, query, key, value, cotangent)
    return pl.pallas_call(
        store_kernel,
        out_shape=(flat,) * 4,
        in_specs=[HBM] * 4,
        out_specs=(HBM,) * 4,
        scratch_shapes=[pltpu.VMEM((4, tokens, features), bf16)]
        + [pltpu.SemaphoreType.DMA((4, 2))] * 2,
        compiler_params=pltpu.CompilerParams(vmem_limit_bytes=60 * 1024 * 1024),
        name="store",
    )(*results)


def solution(mesh):
    rows = P(("groups", "ctx"), None)
    return jax.shard_map(
        per_device,
        mesh=mesh,
        in_specs=(rows, rows, rows, rows, P("groups"), P("groups", None), P("groups", None)),
        out_specs=(rows,) * 4,
        check_vma=False,
    )
```

time: 128 us -> 109 us (0.85)
  the two profiles are of different devices: /device:TPU:0 before, /device:TPU:16 now
where the time goes in v1:
time: 109 us
  Pallas kernels  108 us (99%)
    pallas_call x1, Pallas kernels, per_device(): pl.pallas_call(functools.partial(fused_kernel, count, shares), out_shape=...  106 us
    pallas_call x1, Pallas kernels, per_device(): pl.pallas_call(store_kernel, out_shape=(flat,) * 4, in_specs=[HBM] * 4, o...  2.4 us

profile of v1, /device:TPU:16, one launch (start us, length us, event | category | flops | bytes accessed | tf_op | source)
XLA Modules:
  0.0 108.8 jit_solution(11056692164577861716)
XLA Ops:
  0.6 105.7 %attend.1 = (bf16[256,1024]{1,0:T(8,128)(2,1)}, bf16[256,1024]{1,0:T(8,128)(2,1)}, bf16[256,1024]{1,0:T(8,128)(2,1)}, bf16[256,1024]{1,0:T(8,128)(2,1)}) custom-call(s32[2]{0:T(128)} %glob_hbm.1, s32[6,64]{1,0:T(8,128)} %bitcast.2, s32[6,64]{1,0:T(8,128)} %bitcast.3, bf16[256,1024]{1,0:T(8,128)(2,1)} %q_hbm.1, bf16[256,1024]{1,0:T(8,128)(2,1)} %k_hbm.1, ...), custom_call_target="tpu_custom_call" | custom-call | tf_op jit(solution)/shard_map/attend/pallas_call | solution.py:444
  106.4 2.4 %store.1 = (bf16[256,1024]{1,0:T(8,128)(2,1)}, bf16[256,1024]{1,0:T(8,128)(2,1)}, bf16[256,1024]{1,0:T(8,128)(2,1)}, bf16[256,1024]{1,0:T(8,128)(2,1)}) custom-call(bf16[256,1024]{1,0:T(8,128)(2,1)} %get-tuple-element.8.refs_0_, bf16[256,1024]{1,0:T(8,128)(2,1)} %get-tuple-element.9.refs_1_, bf16[256,1024]{1,0:T(8,128)(2,1)} %get-tuple-element.10.refs_2_, ...), custom_call_target="tpu_custom_call" | custom-call | tf_op jit(solution)/shard_map/store/pallas_call | solution.py:481

commit v2 on v1

--- a/solution.py
+++ b/solution.py
@@ -81,6 +81,23 @@
     my_group = my_head // GROUP_HEADS
     my_rows = pl.ds(pl.multiple_of(my_share * own_tokens, own_tokens), own_tokens)
 
+    def differ(one, other):
+        total, bit = 0, 1
+        while bit < count:
+            total = total + bit * lax.rem(lax.div(one, bit) + lax.div(other, bit), 2)
+            bit *= 2
+        return total
+
+    half = count // 2
+
+    def peer_of(step):
+        step = jnp.int32(step)
+        return differ(me, step // 2 + half * lax.rem(step, 2))
+
+    def step_to(peer):
+        gap = differ(me, peer)
+        return jnp.where(gap >= half, 2 * (gap - half) + 1, 2 * gap)
+
     pulls = [
         pltpu.make_async_copy(source, target, fetch.at[index])
         for index, (source, target) in enumerate(
@@ -101,7 +118,7 @@
         pull.start()
     barrier = pltpu.get_barrier_semaphore()
     for step in range(1, count):
-        peer = lax.rem(me + step, count)
+        peer = peer_of(step)
         pl.semaphore_signal(barrier, inc=1, device_id={"ctx": peer}, device_id_type=MESH)
 
     def pack(left_ref, right_ref, out_ref):
@@ -115,9 +132,6 @@
     pulls[0].wait()
     pulls[1].wait()
     pack(k_ref, v_ref, kv_pack)
-    pulls[2].wait()
-    pulls[3].wait()
-    pack(q_ref, d_ref, qd_pack)
     pl.semaphore_wait(barrier, count - 1)
 
     def kv_copy(dest, came):
@@ -158,9 +172,12 @@
     gkv_copy = row_copy(gkv_put, gkv_got, gkv_out, gkv_in)
 
     for step in range(1, count):
-        kv_copy(lax.rem(me + count - step, count), me).start()
-    for step in range(1, count):
-        qd_copy(lax.rem(me + count - step, count), me).start()
+        kv_copy(peer_of(step), me).start()
+    pulls[2].wait()
+    pulls[3].wait()
+    pack(q_ref, d_ref, qd_pack)
+    for step in range(1, count):
+        qd_copy(peer_of(step), me).start()
 
     for part in range(blocks):
         kv_all[me * blocks + part] = kv_pack[my_head, part * BLOCK : (part + 1) * BLOCK]
@@ -176,7 +193,7 @@
     places = owner_vec[rows, :] * blocks + local_vec[rows, :]
     block_of = lax.broadcasted_iota(jnp.int32, (ROUNDS, all_blocks), 1)
     round_of = lax.broadcasted_iota(jnp.int32, (ROUNDS, all_blocks), 0)
-    turn = lax.rem(lax.div(block_of, blocks) + (count - me), count)
+    turn = step_to(lax.div(block_of, blocks))
     part_of = lax.rem(block_of, blocks) - my_share * own_blocks
     order = (turn * own_blocks + part_of) * ROUNDS + round_of
     order = jnp.where((part_of >= 0) & (part_of < own_blocks), order, -1)
@@ -184,7 +201,7 @@
 
     def link(step, carry):
         before, last = carry
-        peer = lax.rem(me + step, count)
+        peer = peer_of(step)
         for part in range(own_blocks):
             block = peer * blocks + my_share * own_blocks + part
             for kind in range(ROUNDS):
@@ -217,7 +234,7 @@
     to_scalar.wait()
 
     for step in range(1, count):
-        peer = lax.rem(me + step, count)
+        peer = peer_of(step)
         kv_copy(peer, peer).wait_recv()
 
     lane = lax.broadcasted_iota(jnp.int32, (BLOCK, PAIR), 1)
@@ -289,7 +306,7 @@
         ]
 
     def step_of(step, carry):
-        peer = lax.rem(me + step, count)
+        peer = peer_of(step)
 
         @pl.when(step > 0)
         def _():
@@ -316,15 +333,15 @@
 
         @pl.when(step > 1)
         def _():
-            qo_copy(lax.rem(me + step - 1, count), me).start()
+            qo_copy(peer_of(step - 1), me).start()
 
         return carry
 
     lax.fori_loop(0, count, step_of, 0)
-    qo_copy(lax.rem(me + count - 1, count), me).start()
+    qo_copy(peer_of(count - 1), me).start()
 
     def total_of(step, carry):
-        dest = lax.rem(me + count - step, count)
+        dest = peer_of(step)
         for part in range(blocks):
             block = dest * blocks + part
             spot = pl.ds(pl.multiple_of(block * BLOCK, BLOCK), BLOCK)
@@ -343,7 +360,7 @@
     gkv_got[me] = gkv_put[me]
 
     for step in range(1, count):
-        peer = lax.rem(me + step, count)
+        peer = peer_of(step)
         qo_copy(peer, peer).wait_recv()
     for pair in range(heads // 2):
         cols = slice(pair * PAIR, (pair + 1) * PAIR)
@@ -360,7 +377,7 @@
     for push in pushes:
         push.start()
     for step in range(1, count):
-        peer = lax.rem(me + step, count)
+        peer = peer_of(step)
         kv_copy(peer, me).wait_send()
         qd_copy(peer, me).wait_send()
         qo_copy(peer, me).wait_send()
@@ -394,7 +411,7 @@
             push.start()
             pushes.append(push)
     for step in range(1, count):
-        gkv_copy(lax.rem(me + step, count), me).wait_send()
+        gkv_copy(peer_of(step), me).wait_send()
     for push in pushes:
         push.wait()
 

time: 109 us -> 101 us (0.927)
  Pallas kernels: 108 us -> 99.6 us
    pallas_call x1, Pallas kernels: 106 us -> 97.2 us  [per_device(): pl.pallas_call(functools.partial(fused_kernel, count, shares), out_shape=...]
where the time goes in v2:
time: 101 us; the launch traced here: 100 us
  Pallas kernels  99.6 us (99%)
    pallas_call x1, Pallas kernels, per_device(): pl.pallas_call(functools.partial(fused_kernel, count, shares), out_shape=...  97.2 us
    pallas_call x1, Pallas kernels, per_device(): pl.pallas_call(store_kernel, out_shape=(flat,) * 4, in_specs=[HBM] * 4, o...  2.4 us

profile of v2, /device:TPU:16, one launch (start us, length us, event | category | flops | bytes accessed | tf_op | source)
XLA Modules:
  0.0 100.2 jit_solution(2916072777779079629)
XLA Ops:
  0.6 97.2 %attend.1 = (bf16[256,1024]{1,0:T(8,128)(2,1)}, bf16[256,1024]{1,0:T(8,128)(2,1)}, bf16[256,1024]{1,0:T(8,128)(2,1)}, bf16[256,1024]{1,0:T(8,128)(2,1)}) custom-call(s32[2]{0:T(128)} %glob_hbm.1, s32[6,64]{1,0:T(8,128)} %bitcast.2, s32[6,64]{1,0:T(8,128)} %bitcast.3, bf16[256,1024]{1,0:T(8,128)(2,1)} %q_hbm.1, bf16[256,1024]{1,0:T(8,128)(2,1)} %k_hbm.1, ...), custom_call_target="tpu_custom_call" | custom-call | tf_op jit(solution)/shard_map/attend/pallas_call | solution.py:461
  97.8 2.4 %store.1 = (bf16[256,1024]{1,0:T(8,128)(2,1)}, bf16[256,1024]{1,0:T(8,128)(2,1)}, bf16[256,1024]{1,0:T(8,128)(2,1)}, bf16[256,1024]{1,0:T(8,128)(2,1)}) custom-call(bf16[256,1024]{1,0:T(8,128)(2,1)} %get-tuple-element.8.refs_0_, bf16[256,1024]{1,0:T(8,128)(2,1)} %get-tuple-element.9.refs_1_, bf16[256,1024]{1,0:T(8,128)(2,1)} %get-tuple-element.10.refs_2_, ...), custom_call_target="tpu_custom_call" | custom-call | tf_op jit(solution)/shard_map/store/pallas_call | solution.py:498

commit v3 on v2

--- a/solution.py
+++ b/solution.py
@@ -59,7 +59,6 @@
     local_ref,
     table,
     fetch,
-    drain,
     kv_out,
     kv_in,
     qd_out,
@@ -368,14 +367,8 @@
             part = slice(share * own_tokens, (share + 1) * own_tokens)
             even = qo_got[2 * pair * shares + share]
             odd = qo_got[(2 * pair + 1) * shares + share]
-            q_ref[part, cols] = lanes_joined(even[:, :HEAD_DIM], odd[:, :HEAD_DIM])
-            d_ref[part, cols] = lanes_joined(even[:, HEAD_DIM:], odd[:, HEAD_DIM:])
-    pushes = [
-        pltpu.make_async_copy(source, target, fetch.at[place])
-        for place, (source, target) in enumerate(((q_ref, gq_ref), (d_ref, att_ref)))
-    ]
-    for push in pushes:
-        push.start()
+            gq_ref[part, cols] = lanes_joined(even[:, :HEAD_DIM], odd[:, :HEAD_DIM])
+            att_ref[part, cols] = lanes_joined(even[:, HEAD_DIM:], odd[:, HEAD_DIM:])
     for step in range(1, count):
         peer = peer_of(step)
         kv_copy(peer, me).wait_send()
@@ -402,42 +395,25 @@
         cols = slice(pair * PAIR, (pair + 1) * PAIR)
         even = head_of(2 * pair)
         odd = head_of(2 * pair + 1)
-        k_ref[:, cols] = lanes_joined(even[:, :HEAD_DIM], odd[:, :HEAD_DIM])
-        v_ref[:, cols] = lanes_joined(even[:, HEAD_DIM:], odd[:, HEAD_DIM:])
-        for place, (source, target) in enumerate(((k_ref, gk_ref), (v_ref, gv_ref))):
-            push = pltpu.make_async_copy(
-                source.at[:, cols], target.at[:, cols], drain.at[place, pair]
-            )
-            push.start()
-            pushes.append(push)
+        gk_ref[:, cols] = lanes_joined(even[:, :HEAD_DIM], odd[:, :HEAD_DIM])
+        gv_ref[:, cols] = lanes_joined(even[:, HEAD_DIM:], odd[:, HEAD_DIM:])
     for step in range(1, count):
         gkv_copy(peer_of(step), me).wait_send()
+
+
+def store_kernel(*refs):
+    size = (len(refs) - 1) // 2
+    pushes = [
+        pltpu.make_async_copy(refs[index], refs[size + index], refs[-1].at[index])
+        for index in range(size)
+    ]
     for push in pushes:
-        push.wait()
-
-
-def store_kernel(*refs):
-    size = (len(refs) - 3) // 2
-    hold, come, go = refs[2 * size :]
-    half = hold.shape[1] // 2
-    pulls, pushes = [], []
-    for index in range(size):
-        for part in range(2):
-            rows = pl.ds(part * half, half)
-            here = hold.at[index, rows]
-            pulls.append(pltpu.make_async_copy(refs[index].at[rows], here, come.at[index, part]))
-            pushes.append(
-                pltpu.make_async_copy(here, refs[size + index].at[rows], go.at[index, part])
-            )
-    for pull in pulls:
-        pull.start()
-    for pull, push in zip(pulls, pushes):
-        pull.wait()
         push.start()
     for push in pushes:
         push.wait()
 
 
+VMEM = pl.BlockSpec(memory_space=pltpu.VMEM)
 HBM = pl.BlockSpec(memory_space=pltpu.HBM)
 
 
@@ -454,6 +430,10 @@
     shape = jax.ShapeDtypeStruct
     bf16, f32, i32 = jnp.bfloat16, jnp.float32, jnp.int32
 
+    operands = [
+        pltpu.with_memory_space_constraint(operand, pltpu.HBM)
+        for operand in (global_ids, rand_owner.T, rand_local.T, query, key, value, cotangent)
+    ]
     dma = pltpu.SemaphoreType.DMA((count,))
     flat = shape((tokens, features), bf16)
     whole = pltpu.VMEM((tokens, features), bf16)
@@ -462,7 +442,7 @@
         functools.partial(fused_kernel, count, shares),
         out_shape=(flat,) * 4,
         in_specs=[HBM] * 7,
-        out_specs=(HBM,) * 4,
+        out_specs=(VMEM,) * 4,
         scratch_shapes=[
             pltpu.VMEM((heads, tokens, PAIR), bf16),
             pltpu.VMEM((heads, tokens, PAIR), bf16),
@@ -487,22 +467,20 @@
             pltpu.SMEM(index, i32),
             pltpu.SMEM((2 * ROUNDS + 2, all_blocks), i32),
             pltpu.SemaphoreType.DMA((10,)),
-            pltpu.SemaphoreType.DMA((2, heads // 2)),
         ]
         + [dma] * 8,
         compiler_params=pltpu.CompilerParams(
-            collective_id=0, has_side_effects=True, vmem_limit_bytes=60 * 1024 * 1024
+            collective_id=0, has_side_effects=True, vmem_limit_bytes=44 * 1024 * 1024
         ),
         name="attend",
-    )(global_ids, rand_owner.T, rand_local.T, query, key, value, cotangent)
+    )(*operands)
     return pl.pallas_call(
         store_kernel,
         out_shape=(flat,) * 4,
-        in_specs=[HBM] * 4,
+        in_specs=[VMEM] * 4,
         out_specs=(HBM,) * 4,
-        scratch_shapes=[pltpu.VMEM((4, tokens, features), bf16)]
-        + [pltpu.SemaphoreType.DMA((4, 2))] * 2,
-        compiler_params=pltpu.CompilerParams(vmem_limit_bytes=60 * 1024 * 1024),
+        scratch_shapes=[pltpu.SemaphoreType.DMA((4,))],
+        compiler_params=pltpu.CompilerParams(vmem_limit_bytes=1024 * 1024),
         name="store",
     )(*results)
 

time: 101 us -> 99.2 us (0.982)
  Pallas kernels: 99.6 us -> 97.7 us
    pallas_call x1, Pallas kernels: 2.4 us -> 1.35 us  [per_device(): pl.pallas_call(store_kernel, out_shape=(flat,) * 4, in_specs=[VMEM] * 4,...]
where the time goes in v3:
time: 99.2 us; the launch traced here: 98.4 us
  Pallas kernels  97.7 us (98%)
    pallas_call x1, Pallas kernels, per_device(): pl.pallas_call(functools.partial(fused_kernel, count, shares), out_shape=...  96.4 us

profile of v3, /device:TPU:16, one launch (start us, length us, event | category | flops | bytes accessed | tf_op | source)
XLA Modules:
  0.0 98.4 jit_solution(11108453328590041672)
XLA Ops:
  0.6 96.4 %attend.1 = (bf16[256,1024]{1,0:T(8,128)(2,1)S(1)}, bf16[256,1024]{1,0:T(8,128)(2,1)S(1)}, bf16[256,1024]{1,0:T(8,128)(2,1)S(1)}, bf16[256,1024]{1,0:T(8,128)(2,1)S(1)}) custom-call(s32[2]{0:T(128)} %glob_hbm.1, s32[6,64]{1,0:T(8,128)} %bitcast.2, s32[6,64]{1,0:T(8,128)} %bitcast.3, bf16[256,1024]{1,0:T(8,128)(2,1)} %q_hbm.1, bf16[256,1024]{1,0:T(8,128)(2,1)} %k_hbm.1, ...), custom_call_target="tpu_custom_call" | custom-call | tf_op jit(solution)/shard_map/attend/pallas_call | solution.py:441
  97.0 1.3 %store.1 = (bf16[256,1024]{1,0:T(8,128)(2,1)}, bf16[256,1024]{1,0:T(8,128)(2,1)}, bf16[256,1024]{1,0:T(8,128)(2,1)}, bf16[256,1024]{1,0:T(8,128)(2,1)}) custom-call(bf16[256,1024]{1,0:T(8,128)(2,1)S(1)} %get-tuple-element.8.refs_0_, bf16[256,1024]{1,0:T(8,128)(2,1)S(1)} %get-tuple-element.9.refs_1_, bf16[256,1024]{1,0:T(8,128)(2,1)S(1)} %get-tuple-element.10.refs_2_, ...), custom_call_target="tpu_custom_call" | custom-call | tf_op jit(solution)/shard_map/store/pallas_call | solution.py:477

commit v4 on v3

--- a/solution.py
+++ b/solution.py
@@ -59,6 +59,7 @@
     local_ref,
     table,
     fetch,
+    ready,
     kv_out,
     kv_in,
     qd_out,
@@ -97,41 +98,71 @@
         gap = differ(me, peer)
         return jnp.where(gap >= half, 2 * (gap - half) + 1, 2 * gap)
 
-    pulls = [
-        pltpu.make_async_copy(source, target, fetch.at[index])
-        for index, (source, target) in enumerate(
-            (
-                (k_hbm, k_ref),
-                (v_hbm, v_ref),
-                (q_hbm, q_ref),
-                (d_hbm, d_ref),
-                (owner_hbm, owner_ref),
-                (local_hbm, local_ref),
-                (owner_hbm, owner_vec),
-                (local_hbm, local_vec),
-                (glob_hbm, glob_ids),
-            )
-        )
-    ]
-    for pull in pulls:
-        pull.start()
+    quarter = count // 4
+    my_quarter = me // quarter
+    inner = lax.rem(my_quarter + my_quarter // 2, 2)
+    same = [*range(3 * quarter, count), *range(1, quarter)]
+    unlike = [*range(quarter, 3 * quarter)]
+    far = [*range(3 * quarter, count)]
+    mixed = [half * (step % 2) + step // 2 for step in range(1, count)]
+    width = k_ref.shape[2]
+
+    pulls = []
+
+    def pull(source, target):
+        copy = pltpu.make_async_copy(source, target, fetch.at[len(pulls)])
+        copy.start()
+        pulls.append(copy)
+
+    pieces = [differ(my_quarter, jnp.int32(gap)) for gap in (3, 2, 0, 1)]
+    for piece in pieces:
+        cols = pl.ds(pl.multiple_of(piece * width, width), width)
+        pull(k_hbm.at[:, cols], k_ref.at[piece])
+        pull(v_hbm.at[:, cols], v_ref.at[piece])
     barrier = pltpu.get_barrier_semaphore()
-    for step in range(1, count):
-        peer = peer_of(step)
-        pl.semaphore_signal(barrier, inc=1, device_id={"ctx": peer}, device_id_type=MESH)
-
-    def pack(left_ref, right_ref, out_ref):
-        for pair in range(heads // 2):
+
+    def greet(semaphore, gap):
+        pl.semaphore_signal(
+            semaphore, inc=1, device_id={"ctx": differ(me, jnp.int32(gap))}, device_id_type=MESH
+        )
+
+    for gap in same:
+        greet(barrier, gap)
+
+    @pl.when(inner == 1)
+    def _():
+        for gap in unlike:
+            greet(barrier, gap)
+
+    pull(q_hbm, q_ref)
+    pull(d_hbm, d_ref)
+    pull(owner_hbm, owner_ref)
+    pull(local_hbm, local_ref)
+    pull(owner_hbm, owner_vec)
+    pull(local_hbm, local_vec)
+    pull(glob_hbm, glob_ids)
+
+    def pack(left, right, out_ref, head):
+        out_ref[head] = lanes_joined(left[:, :HEAD_DIM], right[:, :HEAD_DIM])
+        out_ref[head + 1] = lanes_joined(left[:, HEAD_DIM:], right[:, HEAD_DIM:])
+
+    def pack_kv(index):
+        pulls[2 * index].wait()
+        pulls[2 * index + 1].wait()
+        piece = pieces[index]
+        for pair in range(heads // 8):
             cols = slice(pair * PAIR, (pair + 1) * PAIR)
-            left = left_ref[:, cols]
-            right = right_ref[:, cols]
-            out_ref[2 * pair] = lanes_joined(left[:, :HEAD_DIM], right[:, :HEAD_DIM])
-            out_ref[2 * pair + 1] = lanes_joined(left[:, HEAD_DIM:], right[:, HEAD_DIM:])
-
-    pulls[0].wait()
-    pulls[1].wait()
-    pack(k_ref, v_ref, kv_pack)
-    pl.semaphore_wait(barrier, count - 1)
+            head = piece * (heads // 4) + 2 * pair
+            pack(k_ref[piece, :, cols], v_ref[piece, :, cols], kv_pack, head)
+
+    pack_kv(0)
+
+    @pl.when(inner == 0)
+    def _():
+        for index in range(1, 4):
+            pack_kv(index)
+
+    pl.semaphore_wait(barrier, 2 * quarter - 1 + (1 - inner) * 2 * quarter)
 
     def kv_copy(dest, came):
         return pltpu.make_async_remote_copy(
@@ -170,11 +201,29 @@
     qo_copy = row_copy(qo_put, qo_got, qo_out, qo_in)
     gkv_copy = row_copy(gkv_put, gkv_got, gkv_out, gkv_in)
 
-    for step in range(1, count):
-        kv_copy(peer_of(step), me).start()
-    pulls[2].wait()
-    pulls[3].wait()
-    pack(q_ref, d_ref, qd_pack)
+    def feed(gaps):
+        for gap in gaps:
+            kv_copy(differ(me, jnp.int32(gap)), me).start()
+
+    @pl.when(inner == 0)
+    def _():
+        for gap in unlike:
+            greet(ready, gap)
+        feed(mixed)
+
+    @pl.when(inner == 1)
+    def _():
+        feed(far)
+        for index in range(1, 4):
+            pack_kv(index)
+        pl.semaphore_wait(ready, 2 * quarter)
+        feed([gap for gap in mixed if gap not in far])
+
+    pulls[8].wait()
+    pulls[9].wait()
+    for pair in range(heads // 2):
+        cols = slice(pair * PAIR, (pair + 1) * PAIR)
+        pack(q_ref[:, cols], d_ref[:, cols], qd_pack, 2 * pair)
     for step in range(1, count):
         qd_copy(peer_of(step), me).start()
 
@@ -185,8 +234,8 @@
     glob_ref[...] = jnp.zeros_like(glob_ref)
     chain_ref[entries] = jnp.zeros_like(chain_ref[entries])
 
-    for pull in pulls[4:]:
-        pull.wait()
+    for copy in pulls[10:]:
+        copy.wait()
     first_row = my_group * ROUNDS
     rows = pl.ds(first_row, ROUNDS)
     places = owner_vec[rows, :] * blocks + local_vec[rows, :]
@@ -391,14 +440,16 @@
             total = total.astype(jnp.bfloat16)
         return total
 
-    for pair in range(heads // 2):
-        cols = slice(pair * PAIR, (pair + 1) * PAIR)
+    for gap in range(heads // 2):
+        if gap == heads // 2 - 1:
+            for step in range(1, count):
+                gkv_copy(peer_of(step), me).wait_send()
+        pair = differ(my_head // 2, jnp.int32(gap))
+        cols = pl.ds(pl.multiple_of(pair * PAIR, PAIR), PAIR)
         even = head_of(2 * pair)
         odd = head_of(2 * pair + 1)
         gk_ref[:, cols] = lanes_joined(even[:, :HEAD_DIM], odd[:, :HEAD_DIM])
         gv_ref[:, cols] = lanes_joined(even[:, HEAD_DIM:], odd[:, HEAD_DIM:])
-    for step in range(1, count):
-        gkv_copy(peer_of(step), me).wait_send()
 
 
 def store_kernel(*refs):
@@ -437,6 +488,7 @@
     dma = pltpu.SemaphoreType.DMA((count,))
     flat = shape((tokens, features), bf16)
     whole = pltpu.VMEM((tokens, features), bf16)
+    cut = pltpu.VMEM((4, tokens, features // 4), bf16)
     index = (rand_owner.shape[1], all_blocks)
     results = pl.pallas_call(
         functools.partial(fused_kernel, count, shares),
@@ -456,8 +508,8 @@
             pltpu.VMEM((entries + 1, BLOCK, PAIR), f32),
             pltpu.VMEM((1 << GLOBALS, BLOCK, PAIR), f32),
             whole,
-            whole,
-            whole,
+            cut,
+            cut,
             whole,
             pltpu.VMEM(index, i32),
             pltpu.VMEM(index, i32),
@@ -466,7 +518,8 @@
             pltpu.SMEM(index, i32),
             pltpu.SMEM(index, i32),
             pltpu.SMEM((2 * ROUNDS + 2, all_blocks), i32),
-            pltpu.SemaphoreType.DMA((10,)),
+            pltpu.SemaphoreType.DMA((16,)),
+            pltpu.SemaphoreType.REGULAR,
         ]
         + [dma] * 8,
         compiler_params=pltpu.CompilerParams(

time: 99.2 us -> 97.8 us (0.986)
  Pallas kernels: 97.7 us -> 96.2 us
    pallas_call x1, Pallas kernels: 96.4 us -> 94.9 us  [per_device(): pl.pallas_call(functools.partial(fused_kernel, count, shares), out_shape=...]
where the time goes in v4:
time: 97.8 us; the launch traced here: 96.9 us
  Pallas kernels  96.2 us (98%)
    pallas_call x1, Pallas kernels, per_device(): pl.pallas_call(functools.partial(fused_kernel, count, shares), out_shape=...  94.9 us

profile of v4, /device:TPU:16, one launch (start us, length us, event | category | flops | bytes accessed | tf_op | source)
XLA Modules:
  0.0 96.9 jit_solution(8415709325850677692)
XLA Ops:
  0.6 94.9 %attend.1 = (bf16[256,1024]{1,0:T(8,128)(2,1)S(1)}, bf16[256,1024]{1,0:T(8,128)(2,1)S(1)}, bf16[256,1024]{1,0:T(8,128)(2,1)S(1)}, bf16[256,1024]{1,0:T(8,128)(2,1)S(1)}) custom-call(s32[2]{0:T(128)} %glob_hbm.1, s32[6,64]{1,0:T(8,128)} %bitcast.2, s32[6,64]{1,0:T(8,128)} %bitcast.3, bf16[256,1024]{1,0:T(8,128)(2,1)} %q_hbm.1, bf16[256,1024]{1,0:T(8,128)(2,1)} %k_hbm.1, ...), custom_call_target="tpu_custom_call" | custom-call | tf_op jit(solution)/shard_map/attend/pallas_call | solution.py:493
  95.5 1.3 %store.1 = (bf16[256,1024]{1,0:T(8,128)(2,1)}, bf16[256,1024]{1,0:T(8,128)(2,1)}, bf16[256,1024]{1,0:T(8,128)(2,1)}, bf16[256,1024]{1,0:T(8,128)(2,1)}) custom-call(bf16[256,1024]{1,0:T(8,128)(2,1)S(1)} %get-tuple-element.8.refs_0_, bf16[256,1024]{1,0:T(8,128)(2,1)S(1)} %get-tuple-element.9.refs_1_, bf16[256,1024]{1,0:T(8,128)(2,1)S(1)} %get-tuple-element.10.refs_2_, ...), custom_call_target="tpu_custom_call" | custom-call | tf_op jit(solution)/shard_map/store/pallas_call | solution.py:530

commit v5 on v4

--- a/solution.py
+++ b/solution.py
@@ -50,6 +50,8 @@
     q_ref,
     k_ref,
     v_ref,
+    k_first,
+    v_first,
     d_ref,
     owner_vec,
     local_vec,
@@ -114,7 +116,14 @@
         copy.start()
         pulls.append(copy)
 
-    pieces = [differ(my_quarter, jnp.int32(gap)) for gap in (3, 2, 0, 1)]
+    team = 2 * shares
+    pairs = [differ(me, jnp.int32(gap)) // team for gap in range(3 * quarter, count, team)]
+    for index, pair in enumerate(pairs):
+        cols = pl.ds(pl.multiple_of(pair * PAIR, PAIR), PAIR)
+        pull(k_hbm.at[:, cols], k_first.at[index])
+        pull(v_hbm.at[:, cols], v_first.at[index])
+    early = len(pulls)
+    pieces = [differ(my_quarter, jnp.int32(gap)) for gap in (2, 0, 1)]
     for piece in pieces:
         cols = pl.ds(pl.multiple_of(piece * width, width), width)
         pull(k_hbm.at[:, cols], k_ref.at[piece])
@@ -147,19 +156,26 @@
         out_ref[head + 1] = lanes_joined(left[:, HEAD_DIM:], right[:, HEAD_DIM:])
 
     def pack_kv(index):
-        pulls[2 * index].wait()
-        pulls[2 * index + 1].wait()
+        pulls[early + 2 * index].wait()
+        pulls[early + 2 * index + 1].wait()
         piece = pieces[index]
         for pair in range(heads // 8):
             cols = slice(pair * PAIR, (pair + 1) * PAIR)
             head = piece * (heads // 4) + 2 * pair
             pack(k_ref[piece, :, cols], v_ref[piece, :, cols], kv_pack, head)
 
-    pack_kv(0)
+    def pack_first(index):
+        pulls[2 * index].wait()
+        pulls[2 * index + 1].wait()
+        pack(k_first[index], v_first[index], kv_pack, 2 * pairs[index])
+
+    pack_first(0)
 
     @pl.when(inner == 0)
     def _():
-        for index in range(1, 4):
+        for index in range(1, len(pairs)):
+            pack_first(index)
+        for index in range(3):
             pack_kv(index)
 
     pl.semaphore_wait(barrier, 2 * quarter - 1 + (1 - inner) * 2 * quarter)
@@ -213,14 +229,18 @@
 
     @pl.when(inner == 1)
     def _():
-        feed(far)
-        for index in range(1, 4):
+        feed(far[:team])
+        for index in range(1, len(pairs)):
+            pack_first(index)
+            feed(far[index * team : (index + 1) * team])
+        for index in range(3):
             pack_kv(index)
         pl.semaphore_wait(ready, 2 * quarter)
         feed([gap for gap in mixed if gap not in far])
 
-    pulls[8].wait()
-    pulls[9].wait()
+    local = early + 6
+    pulls[local].wait()
+    pulls[local + 1].wait()
     for pair in range(heads // 2):
         cols = slice(pair * PAIR, (pair + 1) * PAIR)
         pack(q_ref[:, cols], d_ref[:, cols], qd_pack, 2 * pair)
@@ -234,7 +254,7 @@
     glob_ref[...] = jnp.zeros_like(glob_ref)
     chain_ref[entries] = jnp.zeros_like(chain_ref[entries])
 
-    for copy in pulls[10:]:
+    for copy in pulls[local + 2 :]:
         copy.wait()
     first_row = my_group * ROUNDS
     rows = pl.ds(first_row, ROUNDS)
@@ -489,6 +509,7 @@
     flat = shape((tokens, features), bf16)
     whole = pltpu.VMEM((tokens, features), bf16)
     cut = pltpu.VMEM((4, tokens, features // 4), bf16)
+    first = pltpu.VMEM((heads // 8, tokens, PAIR), bf16)
     index = (rand_owner.shape[1], all_blocks)
     results = pl.pallas_call(
         functools.partial(fused_kernel, count, shares),
@@ -510,6 +531,8 @@
             whole,
             cut,
             cut,
+            first,
+            first,
             whole,
             pltpu.VMEM(index, i32),
             pltpu.VMEM(index, i32),
@@ -518,7 +541,7 @@
             pltpu.SMEM(index, i32),
             pltpu.SMEM(index, i32),
             pltpu.SMEM((2 * ROUNDS + 2, all_blocks), i32),
-            pltpu.SemaphoreType.DMA((16,)),
+            pltpu.SemaphoreType.DMA((2 * (heads // 8) + 14,)),
             pltpu.SemaphoreType.REGULAR,
         ]
         + [dma] * 8,

time: 97.8 us -> 97.7 us (level)
  no operation moved by 1% of the time
where the time goes in v5:
time: 97.7 us; the launch traced here: 96.9 us
  Pallas kernels  96.3 us (99%)
    pallas_call x1, Pallas kernels, per_device(): pl.pallas_call(functools.partial(fused_kernel, count, shares), out_shape=...  94.9 us

profile of v5, /device:TPU:16, one launch (start us, length us, event | category | flops | bytes accessed | tf_op | source)
XLA Modules:
  0.0 96.9 jit_solution(4603000415766789223)
XLA Ops:
  0.6 94.9 %attend.1 = (bf16[256,1024]{1,0:T(8,128)(2,1)S(1)}, bf16[256,1024]{1,0:T(8,128)(2,1)S(1)}, bf16[256,1024]{1,0:T(8,128)(2,1)S(1)}, bf16[256,1024]{1,0:T(8,128)(2,1)S(1)}) custom-call(s32[2]{0:T(128)} %glob_hbm.1, s32[6,64]{1,0:T(8,128)} %bitcast.2, s32[6,64]{1,0:T(8,128)} %bitcast.3, bf16[256,1024]{1,0:T(8,128)(2,1)} %q_hbm.1, bf16[256,1024]{1,0:T(8,128)(2,1)} %k_hbm.1, ...), custom_call_target="tpu_custom_call" | custom-call | tf_op jit(solution)/shard_map/attend/pallas_call | solution.py:514
  95.6 1.3 %store.1 = (bf16[256,1024]{1,0:T(8,128)(2,1)}, bf16[256,1024]{1,0:T(8,128)(2,1)}, bf16[256,1024]{1,0:T(8,128)(2,1)}, bf16[256,1024]{1,0:T(8,128)(2,1)}) custom-call(bf16[256,1024]{1,0:T(8,128)(2,1)S(1)} %get-tuple-element.8.refs_0_, bf16[256,1024]{1,0:T(8,128)(2,1)S(1)} %get-tuple-element.9.refs_1_, bf16[256,1024]{1,0:T(8,128)(2,1)S(1)} %get-tuple-element.10.refs_2_, ...), custom_call_target="tpu_custom_call" | custom-call | tf_op jit(solution)/shard_map/store/pallas_call | solution.py:553

commit v6 on v5

--- a/solution.py
+++ b/solution.py
@@ -399,14 +399,13 @@
                 if mix >> index & 1:
                     glob_ref[mix] += own
 
-        @pl.when(step > 1)
+        @pl.when(step > 0)
         def _():
-            qo_copy(peer_of(step - 1), me).start()
+            qo_copy(peer, me).start()
 
         return carry
 
     lax.fori_loop(0, count, step_of, 0)
-    qo_copy(peer_of(count - 1), me).start()
 
     def total_of(step, carry):
         dest = peer_of(step)

time: 97.7 us -> 97.8 us (level)
  no operation moved by 1% of the time
where the time goes in v6:
time: 97.8 us; the launch traced here: 97 us
  Pallas kernels  96.3 us (98%)
    pallas_call x1, Pallas kernels, per_device(): pl.pallas_call(functools.partial(fused_kernel, count, shares), out_shape=...  95 us

profile of v6, /device:TPU:16, one launch (start us, length us, event | category | flops | bytes accessed | tf_op | source)
XLA Modules:
  0.0 97.0 jit_solution(617524264142895620)
XLA Ops:
  0.6 95.0 %attend.1 = (bf16[256,1024]{1,0:T(8,128)(2,1)S(1)}, bf16[256,1024]{1,0:T(8,128)(2,1)S(1)}, bf16[256,1024]{1,0:T(8,128)(2,1)S(1)}, bf16[256,1024]{1,0:T(8,128)(2,1)S(1)}) custom-call(s32[2]{0:T(128)} %glob_hbm.1, s32[6,64]{1,0:T(8,128)} %bitcast.2, s32[6,64]{1,0:T(8,128)} %bitcast.3, bf16[256,1024]{1,0:T(8,128)(2,1)} %q_hbm.1, bf16[256,1024]{1,0:T(8,128)(2,1)} %k_hbm.1, ...), custom_call_target="tpu_custom_call" | custom-call | tf_op jit(solution)/shard_map/attend/pallas_call | solution.py:513
  95.6 1.3 %store.1 = (bf16[256,1024]{1,0:T(8,128)(2,1)}, bf16[256,1024]{1,0:T(8,128)(2,1)}, bf16[256,1024]{1,0:T(8,128)(2,1)}, bf16[256,1024]{1,0:T(8,128)(2,1)}) custom-call(bf16[256,1024]{1,0:T(8,128)(2,1)S(1)} %get-tuple-element.8.refs_0_, bf16[256,1024]{1,0:T(8,128)(2,1)S(1)} %get-tuple-element.9.refs_1_, bf16[256,1024]{1,0:T(8,128)(2,1)S(1)} %get-tuple-element.10.refs_2_, ...), custom_call_target="tpu_custom_call" | custom-call | tf_op jit(solution)/shard_map/store/pallas_call | solution.py:552
